TPU v7x, 32 devices: a whole 2x2x4 slice. The times are simulated.
32 devices in a mesh: rep: 2 (over x), shard: 16 (over z, y, core).
Axes of the slice: x: 2, y: 2, z: 4, core: 2. Of those that a mesh axis runs over, the one named last changes fastest.
Arguments:
- tokens: bfloat16 [32, 192, 2048], P(('rep', 'shard')), may hold values from -7 to 7
- segment_ids: int32 [32, 192], P(('rep', 'shard')), may hold values from 0 to 3, never falling along the last dimension, each value on 1 to 96 neighbouring positions
- norm_gain: bfloat16 [2048], P('shard'), may hold values from 0.25 to 1.75
- input_weight: bfloat16 [2048, 2048], P('shard'), may hold values from -0.125 to 0.125
- forget_weight: bfloat16 [2048, 2048], P('shard'), may hold values from -0.5 to 0.5
- gate_weight: bfloat16 [2048, 2048], P('shard'), may hold values from -0.125 to 0.125
- mixer_gain: bfloat16 [2048], P('shard'), may hold values from 0.25 to 1.75
- out_weight: bfloat16 [2048, 2048], P('shard'), may hold values from -0.1875 to 0.1875
- ffn_gain: bfloat16 [2048], P('shard'), may hold values from 0.25 to 1.75
- ffn_gate_weight: bfloat16 [2048, 5632], P('shard'), may hold values from -0.125 to 0.125
- ffn_up_weight: bfloat16 [2048, 5632], P('shard'), may hold values from -0.125 to 0.125
- ffn_down_weight: bfloat16 [5632, 2048], P('shard'), may hold values from -0.15625 to 0.15625
- cotangent: bfloat16 [32, 192, 2048], P(('rep', 'shard')), may hold values from -6 to 6
Outputs:
- block_output: bfloat16 [32, 192, 2048], P(('rep', 'shard'))
- input_grad: bfloat16 [32, 192, 2048], P(('rep', 'shard'))
- norm_gain_grad: float32 [2048], P('shard')
- input_weight_grad: float32 [2048, 2048], P('shard')
- forget_weight_grad: float32 [2048, 2048], P('shard')
- gate_weight_grad: float32 [2048, 2048], P('shard')
- mixer_gain_grad: float32 [2048], P('shard')
- out_weight_grad: float32 [2048, 2048], P('shard')
- ffn_gain_grad: float32 [2048], P('shard')
- ffn_gate_grad: float32 [2048, 5632], P('shard')
- ffn_up_grad: float32 [2048, 5632], P('shard')
- ffn_down_grad: float32 [5632, 2048], P('shard')
Inputs may be any that keep to these rules, and one draw needn't show every extreme that they name: `segment_ids`: document numbers never fall along a sequence; each document has 1 to 96 tokens, and one has exactly 96.
All inputs are finite; a program needn't handle non-finite values.
Results may differ from a plain program's by a relative error of at most 0.019.
Values may be sent and summed in bfloat16 or wider, within the bound.
No kernel may reach another device: no remote copies, remote signals or barrier semaphores. Data moves between devices by JAX's collectives and lax.ppermute only.
A program may use at most 640 MiB of HBM per device.

v0:
```python
import jax
import jax.numpy as jnp
from jax import lax
from jax.sharding import PartitionSpec as P

EPSILON = 1e-06


def normalize(values):
    scale = lax.rsqrt(jnp.mean(values * values, axis=-1, keepdims=True) + EPSILON)
    return (values * scale, scale)


def norm_back(grad_scaled, scaled, scale):
    inner = jnp.mean(grad_scaled * scaled, axis=-1, keepdims=True)
    return scale * (grad_scaled - scaled * inner)


def swish_pair(values):
    sigma = jax.nn.sigmoid(values)
    return (values * sigma, sigma * (1.0 + values * (1.0 - sigma)))


def combine_steps(earlier, later):
    return (earlier[0] * later[0], later[0] * earlier[1] + later[1])


def linear_scan(decay, update):
    return lax.associative_scan(combine_steps, (decay, update), axis=0)[1]


def contract_rows(left, piece):
    return lax.dot_general(
        left, piece, (((1,), (1,)), ((), ())), preferred_element_type=jnp.float32
    )


def gain_folder(scaled, carry, pieces):
    sums, fulls, gain_full = carry
    gain_piece = pieces[-1]
    matrices = pieces[:-1]
    columns = scaled * gain_piece.astype(jnp.float32)
    lowered = columns.astype(jnp.bfloat16)
    sums = tuple(
        (jnp.dot(lowered, piece, preferred_element_type=jnp.float32) for piece in matrices)
    )
    gain_full = gain_piece
    return (sums, fulls, gain_full)


def plain_folder(lowered_rows, carry, piece):
    total, full = carry
    total = jnp.dot(lowered_rows, piece, preferred_element_type=jnp.float32)
    return (total, full)


def start_carry(length, width, columns, number):
    sums = tuple((jnp.zeros((length, columns), jnp.float32) for index in range(number)))
    fulls = ()
    return (sums, fulls, jnp.zeros((width,), jnp.bfloat16))


def single_columns(left, piece):
    return contract_rows(left, piece)


def multi_columns(lefts, pieces):
    total = contract_rows(lefts[0], pieces[0])
    for left, piece in zip(lefts[1:], pieces[1:]):
        total = total + contract_rows(left, piece)
    return total


def row_grad(left, right):
    return lax.dot_general(
        left, right, (((0,), (0,)), ((), ())), preferred_element_type=jnp.float32
    )


def row_block(pairs, gains):
    pieces = [row_grad(left, right) for left, right in pairs]
    pieces = pieces + [vector[:, None] for vector in gains]
    return jnp.concatenate(pieces, axis=1)


def shards(
    tokens,
    segment_ids,
    norm_gain,
    input_weight,
    forget_weight,
    gate_weight,
    mixer_gain,
    out_weight,
    ffn_gain,
    ffn_gate_weight,
    ffn_up_weight,
    ffn_down_weight,
    cotangent,
):
    inputs = tokens[0].astype(jnp.float32)
    length, width = inputs.shape
    hidden_width = ffn_up_weight.shape[1]
    segments = segment_ids[0]
    same = jnp.concatenate(
        [jnp.zeros((1,), jnp.float32), (segments[1:] == segments[:-1]).astype(jnp.float32)]
    )
    scaled_in, scale_in = normalize(inputs)
    mixer_sums, mixer_full, gain_one = gain_folder(
        scaled_in,
        start_carry(length, width, width, 3),
        (
            lax.all_gather(input_weight, "shard", axis=0, tiled=True),
            lax.all_gather(forget_weight, "shard", axis=0, tiled=True),
            lax.all_gather(gate_weight, "shard", axis=0, tiled=True),
            lax.all_gather(norm_gain, "shard", axis=0, tiled=True),
        ),
    )
    input_pre, forget_pre, gate_pre = mixer_sums
    forget = jax.nn.sigmoid(forget_pre)
    input_act, input_slope = swish_pair(input_pre)
    update = input_act * (1.0 - forget)
    decay = forget * same[:, None]
    state = linear_scan(decay, update)
    state_scaled, state_scale = normalize(state)
    gate_act, gate_slope = swish_pair(gate_pre)
    mixed_pre = state_scaled * gate_act
    out_sums, out_full, gain_two = gain_folder(
        mixed_pre,
        start_carry(length, width, width, 1),
        (
            lax.all_gather(out_weight, "shard", axis=0, tiled=True),
            lax.all_gather(mixer_gain, "shard", axis=0, tiled=True),
        ),
    )
    resid = inputs + out_sums[0]
    scaled_mid, scale_mid = normalize(resid)
    ffn_sums, ffn_full, gain_three = gain_folder(
        scaled_mid,
        start_carry(length, width, hidden_width, 2),
        (
            lax.all_gather(ffn_gate_weight, "shard", axis=0, tiled=True),
            lax.all_gather(ffn_up_weight, "shard", axis=0, tiled=True),
            lax.all_gather(ffn_gain, "shard", axis=0, tiled=True),
        ),
    )
    ffn_gate, ffn_up = ffn_sums
    ffn_act, ffn_slope = swish_pair(ffn_gate)
    hidden = (ffn_act * ffn_up).astype(jnp.bfloat16)
    down_start = (jnp.zeros((length, width), jnp.float32), jnp.zeros((1, 1), jnp.bfloat16))
    ffn_out, down_full = plain_folder(
        hidden, down_start, lax.all_gather(ffn_down_weight, "shard", axis=0, tiled=True)
    )
    block_output = (resid + ffn_out).astype(jnp.bfloat16)
    grad_out = cotangent[0]
    grad_hidden = single_columns(
        grad_out, lax.all_gather(ffn_down_weight, "shard", axis=0, tiled=True)
    )
    grad_fgate = (grad_hidden * ffn_up * ffn_slope).astype(jnp.bfloat16)
    grad_fup = (grad_hidden * ffn_act).astype(jnp.bfloat16)
    grad_ffn_in = multi_columns(
        (grad_fgate, grad_fup),
        lax.all_gather((ffn_gate_weight, ffn_up_weight), "shard", axis=0, tiled=True),
    )
    gain_three_f = gain_three.astype(jnp.float32)
    mid_low = (scaled_mid * gain_three_f).astype(jnp.bfloat16)
    gain_three_grad = jnp.sum(grad_ffn_in * scaled_mid, axis=0)
    grad_resid = grad_out.astype(jnp.float32) + norm_back(
        grad_ffn_in * gain_three_f, scaled_mid, scale_mid
    )
    grad_branch = grad_resid.astype(jnp.bfloat16)
    grad_mixed = single_columns(
        grad_branch, lax.all_gather(out_weight, "shard", axis=0, tiled=True)
    )
    gain_two_f = gain_two.astype(jnp.float32)
    mixed_low = (mixed_pre * gain_two_f).astype(jnp.bfloat16)
    gain_two_grad = jnp.sum(grad_mixed * mixed_pre, axis=0)
    weighted = grad_mixed * gain_two_f
    grad_gate_pre = (weighted * state_scaled * gate_slope).astype(jnp.bfloat16)
    grad_state = norm_back(weighted * gate_act, state_scaled, state_scale)
    next_decay = jnp.concatenate([decay[1:], jnp.zeros((1, width), jnp.float32)])
    carried = jnp.flip(linear_scan(jnp.flip(next_decay, 0), jnp.flip(grad_state, 0)), 0)
    previous = jnp.concatenate([jnp.zeros((1, width), jnp.float32), state[:-1]])
    grad_forget = carried * previous * same[:, None] - carried * input_act
    grad_input_pre = (carried * (1.0 - forget) * input_slope).astype(jnp.bfloat16)
    grad_forget_pre = (grad_forget * forget * (1.0 - forget)).astype(jnp.bfloat16)
    triple = (grad_input_pre, grad_forget_pre, grad_gate_pre)
    grad_normed = multi_columns(
        triple,
        lax.all_gather((input_weight, forget_weight, gate_weight), "shard", axis=0, tiled=True),
    )
    gain_one_f = gain_one.astype(jnp.float32)
    in_low = (scaled_in * gain_one_f).astype(jnp.bfloat16)
    gain_one_grad = jnp.sum(grad_normed * scaled_in, axis=0)
    input_grad = (grad_resid + norm_back(grad_normed * gain_one_f, scaled_in, scale_in)).astype(
        jnp.bfloat16
    )
    triple_joined = jnp.concatenate(triple, axis=1)
    pair_joined = jnp.concatenate([grad_fgate, grad_fup], axis=1)
    pairs = ((in_low, triple_joined), (mixed_low, grad_branch), (mid_low, pair_joined))
    gains = (gain_one_grad, gain_two_grad, gain_three_grad)
    rows_term = lax.psum_scatter(
        row_block(pairs, gains).astype(jnp.bfloat16), "shard", scatter_dimension=0, tiled=True
    )
    down_term = lax.psum_scatter(
        row_grad(hidden, grad_out).astype(jnp.bfloat16), "shard", scatter_dimension=0, tiled=True
    )
    rows_total, down_total = (
        lax.psum(rows_term, "rep").astype(jnp.float32),
        lax.psum(down_term, "rep").astype(jnp.float32),
    )
    tail = 4 * width + 2 * hidden_width
    return (
        block_output[None],
        input_grad[None],
        rows_total[:, tail],
        rows_total[:, :width],
        rows_total[:, width : 2 * width],
        rows_total[:, 2 * width : 3 * width],
        rows_total[:, tail + 1],
        rows_total[:, 3 * width : 4 * width],
        rows_total[:, tail + 2],
        rows_total[:, 4 * width : 4 * width + hidden_width],
        rows_total[:, 4 * width + hidden_width : tail],
        down_total,
    )


def solution(mesh):
    placed = (
        P(("rep", "shard"), None, None),
        P(("rep", "shard"), None),
        P("shard"),
        P("shard", None),
        P("shard", None),
        P("shard", None),
        P("shard"),
        P("shard", None),
        P("shard"),
        P("shard", None),
        P("shard", None),
        P("shard", None),
        P(("rep", "shard"), None, None),
    )
    return jax.shard_map(
        shards,
        mesh=mesh,
        in_specs=placed,
        out_specs=(
            P(("rep", "shard"), None, None),
            P(("rep", "shard"), None, None),
            P("shard"),
            P("shard", None),
            P("shard", None),
            P("shard", None),
            P("shard"),
            P("shard", None),
            P("shard"),
            P("shard", None),
            P("shard", None),
            P("shard", None),
        ),
        check_vma=False,
    )
```

profile of v0, /device:TPU:0, one launch (start us, length us, event | category | flops | bytes accessed | tf_op | source)
XLA Modules:
  0.0 2012.6 jit_solution(17651145178794768228)
XLA Ops:
  12.0 23.2 %all-gather = bf16[16,1,128]{2,1,0:T(2,128)(2,1)S(1)} all-gather(bf16[1,1,128]{2,1,0:T(2,128)(2,1)S(1)} %bitcast.75), channel_id=1, replica_groups=mesh['rep'=2,'shard'=16] {'shard'}, dimensions={0}, use_global_device_ids=true | all-gather | bytes 4352 | tf_op jit(solution)/shard_map/all_gather | solution.py:116
  35.2 17.5 all-gather.1
  52.7 18.9 all-gather.2
  72.6 15.3 all-gather.11.cloned.1.call-done
  87.9 6.4 fusion.57
  94.3 69.0 %all-gather.13.cloned.1.call-done = bf16[2048,2048]{1,0:T(8,128)(2,1)} async-done(((bf16[128,2048]{1,0:T(8,128)(2,1)}), bf16[2048,2048]{1,0:T(8,128)(2,1)}) %all-gather.13.cloned.1.call-update) | async-done | bytes 8388624 | tf_op jit(solution)/shard_map/all_gather | solution.py:114
  163.3 7.8 broadcast_multiply_fusion
  177.4 4.4 slice.444
  200.5 38.1 %all-gather.15.cloned.1.call-done = bf16[2048,2048]{1,0:T(8,128)(2,1)} async-done(((bf16[128,2048]{1,0:T(8,128)(2,1)}), bf16[2048,2048]{1,0:T(8,128)(2,1)}) %all-gather.15.cloned.1.call-update) | async-done | bytes 8388624 | tf_op jit(solution)/shard_map/all_gather | solution.py:115
  238.6 7.6 multiply_multiply_fusion.1
  246.2 67.6 %all-gather.17.cloned.1.call-done = bf16[2048,2048]{1,0:T(8,128)(2,1)} async-done(((bf16[128,2048]{1,0:T(8,128)(2,1)}), bf16[2048,2048]{1,0:T(8,128)(2,1)}) %all-gather.17.cloned.1.call-update) | async-done | bytes 8388624 | tf_op jit(solution)/shard_map/all_gather | solution.py:132
  313.8 5.9 multiply_reduce_fusion.4
  322.0 110.3 %all-gather.21.cloned.1.call-done = bf16[2048,5632]{1,0:T(8,128)(2,1)} async-done(((bf16[128,5632]{1,0:T(8,128)(2,1)}), bf16[2048,5632]{1,0:T(8,128)(2,1)}) %all-gather.21.cloned.1.call-update) | async-done | bytes 23068688 | tf_op jit(solution)/shard_map/all_gather | solution.py:143
  432.3 14.5 fusion.74
  446.8 105.7 %all-gather.19.cloned.1.call-done = bf16[2048,5632]{1,0:T(8,128)(2,1)} async-done(((bf16[128,5632]{1,0:T(8,128)(2,1)}), bf16[2048,5632]{1,0:T(8,128)(2,1)}) %all-gather.19.cloned.1.call-update) | async-done | bytes 23068688 | tf_op jit(solution)/shard_map/all_gather | solution.py:142
  552.4 14.7 fusion.73
  567.1 105.7 %all-gather.23.cloned.1.call-done = bf16[5632,2048]{1,0:T(8,128)(2,1)} async-done(((bf16[352,2048]{1,0:T(8,128)(2,1)}), bf16[5632,2048]{1,0:T(8,128)(2,1)}) %all-gather.23.cloned.1.call-update) | async-done | bytes 23068688 | tf_op jit(solution)/shard_map/all_gather | solution.py:152
  672.8 16.0 multiply_convert_fusion
  690.1 10.9 convolution_convert_fusion.1
  703.9 4.4 slice.456
  708.3 4.5 slice.449
  712.8 4.5 slice.447
  717.3 8.6 slice.457
  725.9 8.7 slice.448
  734.6 8.6 slice.450
  745.4 12.1 fusion.75
  757.6 14.4 multiply_reduce_fusion
  775.2 8.6 multiply_reduce_fusion.1
  791.4 8.6 slice.452
  800.1 5.1 slice.454
  824.8 5.5 slice.504
  838.6 5.2 pad.115
  846.6 16.0 rev.6
  862.6 4.1 multiply_convert_fusion.4
  866.8 6.8 fusion.76
  873.7 2.9 convolution_add_fusion.1
  876.7 4.3 fusion.24
  882.1 5.8 convolution_convert_fusion.3
  887.9 12.3 copy.30
  900.2 13.6 convolution_convert_fusion.2
  913.7 20.9 %convolution_convert_fusion = bf16[2048,11264]{1,0:T(8,128)(2,1)} fusion(bf16[192,2048]{1,0:T(8,128)(2,1)} %multiply_convert_fusion.6, bf16[192,5632]{1,0:T(8,128)(2,1)} %get-tuple-element.29, bf16[192,5632]{1,0:T(8,128)(2,1)} %get-tuple-element.30), kind=kOutput, calls=%fused_computation | convolution fusion | flops 8890089472 | bytes 51249152 | tf_op jit(solution)/shard_map/dot_general | solution.py:75
  934.6 158.1 %concatenate.84 = bf16[2048,19459]{1,0:T(8,128)(2,1)} concatenate(bf16[2048,6144]{1,0:T(8,128)(2,1)} %convolution_convert_fusion.2, bf16[2048,2048]{1,0:T(8,128)(2,1)} %copy.30, bf16[2048,11264]{1,0:T(8,128)(2,1)} %convolution_convert_fusion, bf16[2048,1]{1,0:T(8,128)(2,1)} %broadcast_in_dim.18, bf16[2048,1]{1,0:T(8,128)(2,1)S(1)} %copy-done.24, bf16[2048,1]{1,0:T(8,128)(2,1)S(1)} %copy-done.25), dimensions={1} | concatenate | bytes 159408128 | tf_op jit(solution)/shard_map/concatenate | solution.py:83
  1092.8 743.0 %reduce-scatter.3.cloned.1.call-done = bf16[128,19459]{1,0:T(8,128)(2,1)} async-done(((bf16[2048,19459]{1,0:T(8,128)(2,1)}), bf16[128,19459]{1,0:T(8,128)(2,1)}) %reduce-scatter.3.cloned.1.call-update) | async-done | bytes 4981520 | tf_op jit(solution)/shard_map/reduce_scatter | solution.py:202
  1835.9 2.9 fusion.28
  1838.7 12.3 fusion.8
  1851.0 143.4 %all-reduce.33.cloned.1.call-done = (bf16[128,19459]{1,0:T(8,128)(2,1)}, bf16[352,2048]{1,0:T(8,128)(2,1)}) async-done(((bf16[128,19459]{1,0:T(8,128)(2,1)}, bf16[352,2048]{1,0:T(8,128)(2,1)}), (bf16[128,19459]{1,0:T(8,128)(2,1)}, bf16[352,2048]{1,0:T(8,128)(2,1)})) %all-reduce.33.cloned.1.call-update) | async-done | bytes 6423312 | tf_op jit(solution)/shard_map/psum | solution.py:209
  1994.4 3.8 fusion.60
  1998.3 3.2 fusion.59
  (310 shorter events, 85.3 us)
Async XLA Ops:
  7.2 80.7 %all-gather.11.cloned.1.call-start = ((), (), s32[]{:S(2)}) async-start(), calls=%async_computation.2 | async-start | bytes 8912896 | tf_op jit(solution)/shard_map/all_gather | solution.py:113
  7.9 155.3 %all-gather.13.cloned.1.call-start = ((), (), s32[]{:S(2)}) async-start(), calls=%async_computation.3 | async-start | bytes 8912896 | tf_op jit(solution)/shard_map/all_gather | solution.py:114
  8.7 229.9 %all-gather.15.cloned.1.call-start = ((), (), s32[]{:S(2)}) async-start(), calls=%async_computation.4 | async-start | bytes 8912896 | tf_op jit(solution)/shard_map/all_gather | solution.py:115
  9.4 304.4 %all-gather.17.cloned.1.call-start = ((), (), s32[]{:S(2)}) async-start(), calls=%async_computation.5 | async-start | bytes 8912896 | tf_op jit(solution)/shard_map/all_gather | solution.py:132
  10.0 422.3 %all-gather.21.cloned.1.call-start = ((), (), s32[]{:S(2)}) async-start(), calls=%async_computation.7 | async-start | bytes 24510464 | tf_op jit(solution)/shard_map/all_gather | solution.py:143
  10.6 24.7 %copy-start.46 = (bf16[128]{0:T(256)(128)(2,1)S(1)}, bf16[128]{0:T(256)(128)(2,1)}, u32[]{:S(2)}) copy-start(bf16[128]{0:T(256)(128)(2,1)} %param.19) | copy-start | bytes 772
  10.6 42.1 %copy-start.47 = (bf16[128]{0:T(256)(128)(2,1)S(1)}, bf16[128]{0:T(256)(128)(2,1)}, u32[]{:S(2)}) copy-start(bf16[128]{0:T(256)(128)(2,1)} %param.21) | copy-start | bytes 772
  10.6 61.6 %copy-start.44 = (s32[1,192]{1,0:T(1,128)S(1)}, s32[1,192]{1,0:T(1,128)}, u32[]{:S(2)}) copy-start(s32[1,192]{1,0:T(1,128)} %param.14) | copy-start | bytes 2308
  10.6 61.8 %copy-start.1 = (bf16[1,192,2048]{2,1,0:T(8,128)(2,1)S(1)}, bf16[1,192,2048]{2,1,0:T(8,128)(2,1)}, u32[]{:S(2)}) copy-start(bf16[1,192,2048]{2,1,0:T(8,128)(2,1)} %param.13) | copy-start | bytes 2359300
  10.6 541.8 %all-gather.19.cloned.1.call-start = ((), (), s32[]{:S(2)}) async-start(), calls=%async_computation.6 | async-start | bytes 24510464 | tf_op jit(solution)/shard_map/all_gather | solution.py:142
  11.2 661.6 %all-gather.23.cloned.1.call-start = ((), (), s32[]{:S(2)}) async-start(), calls=%async_computation.8 | async-start | bytes 24510464 | tf_op jit(solution)/shard_map/all_gather | solution.py:152
  11.9 1080.8 %reduce-scatter.5.cloned.1.call-start = ((), (), s32[]{:S(2)}) async-start(), calls=%async_computation.10 | async-start | bytes 24510464 | tf_op jit(solution)/shard_map/reduce_scatter | solution.py:205
  72.4 90.9 %copy-start.42 = (f32[192]{0:T(256)}, f32[192]{0:T(256)S(1)}, u32[]{:S(2)}) copy-start(f32[192]{0:T(256)S(1)} %add_convert_fusion) | copy-start | bytes 2308
  72.6 90.6 %copy-start.32 = (f32[192]{0:T(256)}, f32[192]{0:T(256)S(1)}, u32[]{:S(2)}) copy-start(f32[192]{0:T(256)S(1)} %add_rsqrt_fusion.2) | copy-start | bytes 2308
  171.0 2.6 copy-start.3
  175.9 6.0 copy-start.10
  181.9 4.3 copy-start.13
  194.1 1.6 copy-start.18
  199.1 39.5 %copy-start.33 = (f32[192]{0:T(256)S(1)}, f32[192]{0:T(256)}, u32[]{:S(2)}) copy-start(f32[192]{0:T(256)} %copy-done.32) | copy-start | bytes 2308
  313.8 7.1 copy-start.31
  672.8 17.3 copy-start.20
  701.1 1134.7 %reduce-scatter.3.cloned.1.call-start = ((), (), s32[]{:S(2)}) async-start(), calls=%async_computation.9 | async-start | bytes 85229568 | tf_op jit(solution)/shard_map/reduce_scatter | solution.py:202
  743.2 2.2 copy-start.23
  745.4 12.2 copy-start.6
  772.0 2.2 copy-start.4
  772.0 2.7 copy-start.21
  772.0 3.2 copy-start.27
  791.4 8.7 copy-start.15
  810.3 3.6 copy-start.26
  819.0 5.8 copy-start.14
  822.9 7.7 copy-start.41
  832.9 1.7 copy-start.19
  846.6 16.0 copy-start.43
  862.6 11.0 slice-start
  866.8 6.9 copy-start.12
  866.8 6.9 slice-start.1
  866.8 9.8 slice-start.2
  873.7 2.9 copy-start.2
  873.7 2.9 slice-start.3
  873.7 2.9 copy-start.11
  873.7 2.9 copy-start.34
  876.6 5.4 copy-start.22
  913.7 20.9 %copy-start.24 = (bf16[2048,1]{1,0:T(8,128)(2,1)S(1)}, bf16[2048,1]{1,0:T(8,128)(2,1)}, u32[]{:S(2)}) copy-start(bf16[2048,1]{1,0:T(8,128)(2,1)} %broadcast_in_dim.19) | copy-start | bytes 12292
  913.7 20.9 %copy-start.25 = (bf16[2048,1]{1,0:T(8,128)(2,1)S(1)}, bf16[2048,1]{1,0:T(8,128)(2,1)}, u32[]{:S(2)}) copy-start(bf16[2048,1]{1,0:T(8,128)(2,1)} %broadcast_in_dim.20) | copy-start | bytes 12292
  1092.7 901.7 %all-reduce.33.cloned.1.call-start = ((), (), s32[]{:S(2)}) async-start(), calls=%async_computation.11 | async-start | bytes 12910592 | tf_op jit(solution)/shard_map/psum | solution.py:209
  1835.8 2.9 copy-start.7
  1835.9 2.9 copy-start.9
  1994.4 3.9 copy-start
  (14 other events, 14.5 us)
Sparse Core Ops, SparseCore 0:
  10.2 77.6 all-gather.10
  90.1 73.1 all-gather.12
  165.4 73.1 all-gather.14
  240.6 73.1 all-gather.16
  315.3 116.9 all-gather.20
  433.7 118.6 all-gather.18
  554.0 118.6 all-gather.22
  701.2 226.8 reduce-scatter.4
  1092.8 742.9 reduce-scatter.2
  1838.2 156.2 all-reduce.32
where the time goes:
time: 2030 us; the launch traced here: 2010 us
  waiting for transfers between devices  1400 us (69%)
  local copies, waits for them, and re-layouts  319 us (16%)
  matrix products  185 us (9%)
  blocking collectives  59.6 us (3%)
  other arithmetic  30.4 us (1%)
    reduce_scatter x1, waiting for transfers between devices, shards(): lax.psum_scatter(row_block(pairs, gains).astype(jnp.bfloat16), 'shard', s...  743 us
    concatenate x1, local copies, waits for them, and re-layouts, row_block(): return jnp.concatenate(pieces, axis=1)  158 us
    psum x1, waiting for transfers between devices, shards(): lax.psum(rows_term, 'rep').astype(jnp.float32)  143 us
    all_gather x1, waiting for transfers between devices, shards(): lax.all_gather(ffn_up_weight, 'shard', axis=0, tiled=True)  110 us
    all_gather x1, waiting for transfers between devices, shards(): lax.all_gather(ffn_gate_weight, 'shard', axis=0, tiled=True)  106 us
    all_gather x1, waiting for transfers between devices, shards(): lax.all_gather(ffn_down_weight, 'shard', axis=0, tiled=True)  106 us
    slice x90, local copies, waits for them, and re-layouts, linear_scan(): return lax.associative_scan(combine_steps, (decay, update), axis=0)[1]  96.4 us
    all_gather x1, waiting for transfers between devices, shards(): lax.all_gather(forget_weight, 'shard', axis=0, tiled=True)  69 us
  transfers between devices with their start and end apart: 10, of which 9 were waited for; matrix products, arithmetic and copies ran while one was open for 24% of the time, Pallas kernels for 0%

commit v1 on v0

--- a/solution.py
+++ b/solution.py
@@ -4,6 +4,12 @@
 from jax.sharding import PartitionSpec as P
 
 EPSILON = 1e-06
+
+
+def do_roads(sheet, d0):
+    p_next = list(sheet.shape[1:])
+    p_next[d0] *= sheet.shape[0]
+    return jnp.moveaxis(sheet, 0, d0).reshape(p_next)
 
 
 def normalize(values):
@@ -135,12 +141,39 @@
     )
     resid = inputs + out_sums[0]
     scaled_mid, scale_mid = normalize(resid)
+
+    def pieces_all_obtain(v0, axis_key, dimension_no):
+        amount_of = lax.axis_size(axis_key)
+        in_order = []
+        it = 0
+        while it < amount_of:
+            in_order.append((it, (it + 1) % amount_of))
+            it += 1
+        line_up = []
+        for c, dev_j in in_order:
+            line_up.append((dev_j, c))
+        t1, inter = ([], [])
+        b = 0
+        while b < amount_of - 1:
+            if b % 2 == 0:
+                t1.append(lax.ppermute(t1[-1] if t1 else v0, axis_key, perm=in_order))
+            else:
+                mixed_arr = lax.ppermute(inter[-1] if inter else v0, axis_key, perm=line_up)
+                inter.append(mixed_arr)
+            b = b + 1
+        res = jnp.stack([*t1[::-1], v0, *inter])
+        small = lax.axis_index(axis_key)
+        s_next = len(t1)
+        built = small - s_next
+        res = res[(jnp.arange(amount_of) - built) % amount_of]
+        return do_roads(res, dimension_no)
+
     ffn_sums, ffn_full, gain_three = gain_folder(
         scaled_mid,
         start_carry(length, width, hidden_width, 2),
         (
             lax.all_gather(ffn_gate_weight, "shard", axis=0, tiled=True),
-            lax.all_gather(ffn_up_weight, "shard", axis=0, tiled=True),
+            pieces_all_obtain(ffn_up_weight, "shard", 0),
             lax.all_gather(ffn_gain, "shard", axis=0, tiled=True),
         ),
     )

time: 2030 us -> 2140 us (1.054)
  waiting for transfers between devices: 1400 us -> 1230 us
  local copies, waits for them, and re-layouts: 319 us -> 466 us
  starting transfers between devices: 0.39 us -> 88.5 us
  other arithmetic: 30.4 us -> 53.5 us
    ppermute x0 -> x15, waiting for transfers between devices: none -> 189 us  [the longest x8 188 us: pieces_all_obtain(): t1.append(lax.ppermute(t1[-1] if t1 else v0, axis_key, perm=in_order))]
    slice x90, local copies, waits for them, and re-layouts: 96.4 us -> 194 us  [linear_scan(): return lax.associative_scan(combine_steps, (decay, update), axis=0)[1]]
    ppermute x0 -> x15, starting transfers between devices: none -> 88.1 us  [the longest x8 77.2 us: pieces_all_obtain(): t1.append(lax.ppermute(t1[-1] if t1 else v0, axis_key, perm=in_order))]
    all_gather x1, waiting for transfers between devices: 110 us -> 24.3 us  [shards(): lax.all_gather((ffn_gate_weight, ffn_up_weight), 'shard', axis=0, tiled=T...]
    all_gather x1, waiting for transfers between devices: 106 us -> 24.4 us  [shards(): lax.all_gather(ffn_down_weight, 'shard', axis=0, tiled=True)]
    all_gather x1, waiting for transfers between devices: 69 us -> 0.01 us  [shards(): lax.all_gather(forget_weight, 'shard', axis=0, tiled=True)]
    all_gather x1, waiting for transfers between devices: 67.6 us -> 0.01 us  [shards(): lax.all_gather(out_weight, 'shard', axis=0, tiled=True)]
    all_gather x1, waiting for transfers between devices: 38.1 us -> 0.01 us  [shards(): lax.all_gather(gate_weight, 'shard', axis=0, tiled=True)]
  transfers between devices with their start and end apart: 10 -> 25, of which waited for: 9 -> 13; matrix products, arithmetic and copies ran while one was open for 24% -> 32% of each run, Pallas kernels for 0% -> 0%
where the time goes in v1:
time: 2140 us; the launch traced here: 2120 us
  waiting for transfers between devices  1230 us (57%)
  local copies, waits for them, and re-layouts  466 us (22%)
  matrix products  184 us (9%)
  starting transfers between devices  88.5 us (4%)
  blocking collectives  80.3 us (4%)
  other arithmetic  53.5 us (2%)
    reduce_scatter x1, waiting for transfers between devices, shards(): lax.psum_scatter(row_block(pairs, gains).astype(jnp.bfloat16), 'shard', s...  743 us
    slice x90, local copies, waits for them, and re-layouts, linear_scan(): return lax.associative_scan(combine_steps, (decay, update), axis=0)[1]  194 us
    ppermute x8, waiting for transfers between devices, pieces_all_obtain(): t1.append(lax.ppermute(t1[-1] if t1 else v0, axis_key, perm=in_order))  188 us
    concatenate x1, local copies, waits for them, and re-layouts, row_block(): return jnp.concatenate(pieces, axis=1)  158 us
    psum x1, waiting for transfers between devices, shards(): lax.psum(rows_term, 'rep').astype(jnp.float32)  143 us
    all_gather x1, waiting for transfers between devices, shards(): lax.all_gather(ffn_gate_weight, 'shard', axis=0, tiled=True)  107 us
    ppermute x8, starting transfers between devices, pieces_all_obtain(): t1.append(lax.ppermute(t1[-1] if t1 else v0, axis_key, perm=in_order))  77.2 us
    dot_general x7, matrix products, contract_rows(): lax.dot_general(left, piece, (((1,), (1,)), ((), ())), preferred_element_...  64.6 us
  transfers between devices with their start and end apart: 25, of which 13 were waited for; matrix products, arithmetic and copies ran while one was open for 32% of the time, Pallas kernels for 0%

profile of v1, /device:TPU:0, one launch (start us, length us, event | category | flops | bytes accessed | tf_op | source)
XLA Modules:
  0.0 2122.1 jit_solution(1491676523445934297)
XLA Ops:
  11.8 35.1 %collective-permute-done = bf16[128,5632]{1,0:T(8,128)(2,1)S(1)} collective-permute-done((bf16[128,5632]{1,0:T(8,128)(2,1)S(1)}, bf16[128,5632]{1,0:T(8,128)(2,1)S(1)}, u32[]{:S(2)}, u32[]{:S(2)}) %collective-permute-start) | collective-permute-done | bytes 1441824 | tf_op jit(solution)/shard_map/ppermute | solution.py:159
  51.3 34.5 %collective-permute-done.1 = bf16[128,5632]{1,0:T(8,128)(2,1)S(1)} collective-permute-done((bf16[128,5632]{1,0:T(8,128)(2,1)S(1)}, bf16[128,5632]{1,0:T(8,128)(2,1)S(1)}, u32[]{:S(2)}, u32[]{:S(2)}) %collective-permute-start.1) | collective-permute-done | bytes 1441824 | tf_op jit(solution)/shard_map/ppermute | solution.py:159
  90.3 16.7 collective-permute-done.2
  107.1 16.2 collective-permute-start.3
  123.3 25.2 %collective-permute-done.3 = bf16[128,5632]{1,0:T(8,128)(2,1)S(1)} collective-permute-done((bf16[128,5632]{1,0:T(8,128)(2,1)S(1)}, bf16[128,5632]{1,0:T(8,128)(2,1)S(1)}, u32[]{:S(2)}, u32[]{:S(2)}) %collective-permute-start.3) | collective-permute-done | bytes 1441824 | tf_op jit(solution)/shard_map/ppermute | solution.py:159
  148.5 8.4 collective-permute-start.4
  158.0 24.6 %collective-permute-done.4 = bf16[128,5632]{1,0:T(8,128)(2,1)S(1)} collective-permute-done((bf16[128,5632]{1,0:T(8,128)(2,1)S(1)}, bf16[128,5632]{1,0:T(8,128)(2,1)S(1)}, u32[]{:S(2)}, u32[]{:S(2)}) %collective-permute-start.4) | collective-permute-done | bytes 1441824 | tf_op jit(solution)/shard_map/ppermute | solution.py:159
  182.6 12.2 collective-permute-start.5
  196.2 28.1 %collective-permute-done.5 = bf16[128,5632]{1,0:T(8,128)(2,1)S(1)} collective-permute-done((bf16[128,5632]{1,0:T(8,128)(2,1)S(1)}, bf16[128,5632]{1,0:T(8,128)(2,1)S(1)}, u32[]{:S(2)}, u32[]{:S(2)}) %collective-permute-start.5) | collective-permute-done | bytes 1441824 | tf_op jit(solution)/shard_map/ppermute | solution.py:159
  224.3 25.5 %collective-permute-start.6 = (bf16[128,5632]{1,0:T(8,128)(2,1)S(1)}, bf16[128,5632]{1,0:T(8,128)(2,1)}, u32[]{:S(2)}, u32[]{:S(2)}) collective-permute-start(bf16[128,5632]{1,0:T(8,128)(2,1)S(1)} %collective-permute-done.5), channel_id=1, source_target_pairs={{0,1},{1,2},{2,3},{3,4},{4,5},{5,6},{6,7},{7,8},{8,9},{9,10},{10,1... | collective-permute-start | bytes 4325384 | tf_op jit(solution)/shard_map/ppermute | solution.py:159
  251.0 23.9 %collective-permute-done.6 = bf16[128,5632]{1,0:T(8,128)(2,1)} collective-permute-done((bf16[128,5632]{1,0:T(8,128)(2,1)S(1)}, bf16[128,5632]{1,0:T(8,128)(2,1)}, u32[]{:S(2)}, u32[]{:S(2)}) %collective-permute-start.6) | collective-permute-done | bytes 1441824 | tf_op jit(solution)/shard_map/ppermute | solution.py:159
  274.9 14.4 collective-permute-start.7
  289.8 42.9 %all-gather = bf16[16,1,128]{2,1,0:T(2,128)(2,1)S(1)} all-gather(bf16[1,1,128]{2,1,0:T(2,128)(2,1)S(1)} %bitcast.109), channel_id=1, replica_groups=mesh['rep'=2,'shard'=16] {'shard'}, dimensions={0}, use_global_device_ids=true | all-gather | bytes 4352 | tf_op jit(solution)/shard_map/all_gather | solution.py:122
  332.7 20.1 all-gather.1
  352.9 17.3 all-gather.2
  403.6 17.5 gather_fusion
  421.1 6.5 fusion.59
  427.6 8.1 broadcast_multiply_fusion
  442.4 4.6 slice.444
  522.9 7.8 multiply_multiply_fusion.1
  530.7 6.2 multiply_reduce_fusion.4
  539.1 24.4 %all-gather.21.cloned.1.call-done = bf16[5632,2048]{1,0:T(8,128)(2,1)} async-done(((bf16[352,2048]{1,0:T(8,128)(2,1)}), bf16[5632,2048]{1,0:T(8,128)(2,1)}) %all-gather.21.cloned.1.call-update) | async-done | bytes 23068688 | tf_op jit(solution)/shard_map/all_gather | solution.py:185
  563.5 13.6 fusion.32
  577.1 106.6 %all-gather.19.cloned.1.call-done = bf16[2048,5632]{1,0:T(8,128)(2,1)} async-done(((bf16[128,5632]{1,0:T(8,128)(2,1)}), bf16[2048,5632]{1,0:T(8,128)(2,1)}) %all-gather.19.cloned.1.call-update) | async-done | bytes 23068688 | tf_op jit(solution)/shard_map/all_gather | solution.py:175
  683.7 12.7 fusion.75
  696.4 14.5 multiply_convert_fusion
  712.2 11.2 convolution_convert_fusion.1
  739.4 8.6 slice.448
  748.0 8.5 slice.457
  756.5 8.6 slice.450
  767.3 12.4 fusion.76
  779.7 24.3 %all-gather.23.cloned.1.call-done = bf16[2048,5632]{1,0:T(8,128)(2,1)} async-done(((bf16[128,5632]{1,0:T(8,128)(2,1)}), bf16[2048,5632]{1,0:T(8,128)(2,1)}) %all-gather.23.cloned.1.call-update) | async-done | bytes 23068688 | tf_op jit(solution)/shard_map/all_gather | solution.py:196
  804.0 14.3 multiply_reduce_fusion
  823.1 10.4 multiply_reduce_fusion.1
  840.6 8.6 slice.454
  849.2 8.6 slice.452
  927.2 9.0 slice.504
  945.1 5.2 pad.115
  953.1 16.2 rev.6
  969.3 5.8 convolution_convert_fusion.3
  975.1 12.4 copy.30
  991.6 6.6 fusion.77
  1009.0 13.5 convolution_convert_fusion.2
  1022.6 21.0 convolution_convert_fusion
  1043.6 158.0 %concatenate.84 = bf16[2048,19459]{1,0:T(8,128)(2,1)} concatenate(bf16[2048,6144]{1,0:T(8,128)(2,1)} %convolution_convert_fusion.2, bf16[2048,2048]{1,0:T(8,128)(2,1)} %copy.30, bf16[2048,11264]{1,0:T(8,128)(2,1)} %convolution_convert_fusion, bf16[2048,1]{1,0:T(8,128)(2,1)S(1)} %copy-done.24, bf16[2048,1]{1,0:T(8,128)(2,1)S(1)} %copy-done.25, bf16[2048,1]{1,0:T(8,128)(2,1)} %broadcast_in_dim.20), dimensions={1} | concatenate | bytes 159408128 | tf_op jit(solution)/shard_map/concatenate | solution.py:89
  1201.7 742.8 %reduce-scatter.3.cloned.1.call-done = bf16[128,19459]{1,0:T(8,128)(2,1)} async-done(((bf16[2048,19459]{1,0:T(8,128)(2,1)}), bf16[128,19459]{1,0:T(8,128)(2,1)}) %reduce-scatter.3.cloned.1.call-update) | async-done | bytes 4981520 | tf_op jit(solution)/shard_map/reduce_scatter | solution.py:235
  1947.5 12.3 fusion.8
  1959.7 143.4 %all-reduce.33.cloned.1.call-done = (bf16[128,19459]{1,0:T(8,128)(2,1)}, bf16[352,2048]{1,0:T(8,128)(2,1)}) async-done(((bf16[128,19459]{1,0:T(8,128)(2,1)}, bf16[352,2048]{1,0:T(8,128)(2,1)}), (bf16[128,19459]{1,0:T(8,128)(2,1)}, bf16[352,2048]{1,0:T(8,128)(2,1)})) %all-reduce.33.cloned.1.call-update) | async-done | bytes 6423312 | tf_op jit(solution)/shard_map/psum | solution.py:242
  (433 shorter events, 277.3 us)
Async XLA Ops:
  7.2 413.9 %all-gather.11.cloned.1.call-start = ((), (), s32[]{:S(2)}) async-start(), calls=%async_computation.2 | async-start | bytes 8912896 | tf_op jit(solution)/shard_map/all_gather | solution.py:119
  7.9 419.7 %all-gather.13.cloned.1.call-start = ((), (), s32[]{:S(2)}) async-start(), calls=%async_computation.3 | async-start | bytes 8912896 | tf_op jit(solution)/shard_map/all_gather | solution.py:120
  8.7 514.2 %all-gather.15.cloned.1.call-start = ((), (), s32[]{:S(2)}) async-start(), calls=%async_computation.4 | async-start | bytes 8912896 | tf_op jit(solution)/shard_map/all_gather | solution.py:121
  9.4 521.3 %all-gather.17.cloned.1.call-start = ((), (), s32[]{:S(2)}) async-start(), calls=%async_computation.5 | async-start | bytes 8912896 | tf_op jit(solution)/shard_map/all_gather | solution.py:138
  10.0 553.5 %all-gather.21.cloned.1.call-start = ((), (), s32[]{:S(2)}) async-start(), calls=%async_computation.7 | async-start | bytes 24510464 | tf_op jit(solution)/shard_map/all_gather | solution.py:185
  10.6 278.8 %copy-start.81 = (s32[1,192]{1,0:T(1,128)S(1)}, s32[1,192]{1,0:T(1,128)}, u32[]{:S(2)}) copy-start(s32[1,192]{1,0:T(1,128)} %param.14) | copy-start | bytes 2308
  10.6 278.9 %copy-start.1 = (bf16[1,192,2048]{2,1,0:T(8,128)(2,1)S(1)}, bf16[1,192,2048]{2,1,0:T(8,128)(2,1)}, u32[]{:S(2)}) copy-start(bf16[1,192,2048]{2,1,0:T(8,128)(2,1)} %param.13) | copy-start | bytes 2359300
  10.6 279.2 %copy-start.82 = (bf16[128]{0:T(256)(128)(2,1)S(1)}, bf16[128]{0:T(256)(128)(2,1)}, u32[]{:S(2)}) copy-start(bf16[128]{0:T(256)(128)(2,1)} %param.15) | copy-start | bytes 772
  10.6 322.1 %copy-start.83 = (bf16[128]{0:T(256)(128)(2,1)S(1)}, bf16[128]{0:T(256)(128)(2,1)}, u32[]{:S(2)}) copy-start(bf16[128]{0:T(256)(128)(2,1)} %param.19) | copy-start | bytes 772
  10.6 342.3 %copy-start.84 = (bf16[128]{0:T(256)(128)(2,1)S(1)}, bf16[128]{0:T(256)(128)(2,1)}, u32[]{:S(2)}) copy-start(bf16[128]{0:T(256)(128)(2,1)} %param.21) | copy-start | bytes 772
  10.6 673.0 %all-gather.19.cloned.1.call-start = ((), (), s32[]{:S(2)}) async-start(), calls=%async_computation.6 | async-start | bytes 24510464 | tf_op jit(solution)/shard_map/all_gather | solution.py:175
  11.2 792.8 %all-gather.23.cloned.1.call-start = ((), (), s32[]{:S(2)}) async-start(), calls=%async_computation.8 | async-start | bytes 24510464 | tf_op jit(solution)/shard_map/all_gather | solution.py:196
  11.3 35.6 %collective-permute-start = (bf16[128,5632]{1,0:T(8,128)(2,1)S(1)}, bf16[128,5632]{1,0:T(8,128)(2,1)S(1)}, u32[]{:S(2)}, u32[]{:S(2)}) collective-permute-start(bf16[128,5632]{1,0:T(8,128)(2,1)S(1)} %copy-done.8), channel_id=1, source_target_pairs={{0,1},{1,2},{2,3},{3,4},{4,5},{5,6},{6,7},{7,8},{8,9},{9,10},{10,1... | collective-permute-start | bytes 4325384 | tf_op jit(solution)/shard_map/ppermute | solution.py:159
  46.8 39.0 %copy-start.28 = (bf16[128,5632]{1,0:T(8,128)(2,1)}, bf16[128,5632]{1,0:T(8,128)(2,1)S(1)}, u32[]{:S(2)}) copy-start(bf16[128,5632]{1,0:T(8,128)(2,1)S(1)} %collective-permute-done) | copy-start | bytes 4325380
  46.8 39.0 %collective-permute-start.1 = (bf16[128,5632]{1,0:T(8,128)(2,1)S(1)}, bf16[128,5632]{1,0:T(8,128)(2,1)S(1)}, u32[]{:S(2)}, u32[]{:S(2)}) collective-permute-start(bf16[128,5632]{1,0:T(8,128)(2,1)S(1)} %collective-permute-done), channel_id=1, source_target_pairs={{0,1},{1,2},{2,3},{3,4},{4,5},{5,6},{6,7},{7,8},{8,9},{9,10},{10,1... | collective-permute-start | bytes 4325384 | tf_op jit(solution)/shard_map/ppermute | solution.py:159
  46.8 39.0 %collective-permute-start.8 = (bf16[128,5632]{1,0:T(8,128)(2,1)S(1)}, bf16[128,5632]{1,0:T(8,128)(2,1)S(1)}, u32[]{:S(2)}, u32[]{:S(2)}) collective-permute-start(bf16[128,5632]{1,0:T(8,128)(2,1)S(1)} %copy-done.8), channel_id=1, source_target_pairs={{1,0},{2,1},{3,2},{4,3},{5,4},{6,5},{7,6},{8,7},{9,8},{10,9},{11,1... | collective-permute-start | bytes 4325384 | tf_op jit(solution)/shard_map/ppermute | solution.py:161
  85.8 37.4 %copy-start.32 = (bf16[128,5632]{1,0:T(8,128)(2,1)}, bf16[128,5632]{1,0:T(8,128)(2,1)S(1)}, u32[]{:S(2)}) copy-start(bf16[128,5632]{1,0:T(8,128)(2,1)S(1)} %collective-permute-done.1) | copy-start | bytes 4325380
  85.8 21.2 %collective-permute-start.2 = (bf16[128,5632]{1,0:T(8,128)(2,1)S(1)}, bf16[128,5632]{1,0:T(8,128)(2,1)S(1)}, u32[]{:S(2)}, u32[]{:S(2)}) collective-permute-start(bf16[128,5632]{1,0:T(8,128)(2,1)S(1)} %collective-permute-done.1), channel_id=1, source_target_pairs={{0,1},{1,2},{2,3},{3,4},{4,5},{5,6},{6,7},{7,8},{8,9},{9,10},{10,1... | collective-permute-start | bytes 4325384 | tf_op jit(solution)/shard_map/ppermute | solution.py:159
  85.8 37.4 %collective-permute-start.9 = (bf16[128,5632]{1,0:T(8,128)(2,1)S(1)}, bf16[128,5632]{1,0:T(8,128)(2,1)S(1)}, u32[]{:S(2)}, u32[]{:S(2)}) collective-permute-start(bf16[128,5632]{1,0:T(8,128)(2,1)S(1)} %collective-permute-done.8), channel_id=1, source_target_pairs={{1,0},{2,1},{3,2},{4,3},{5,4},{6,5},{7,6},{8,7},{9,8},{10,9},{11,1... | collective-permute-start | bytes 4325384 | tf_op jit(solution)/shard_map/ppermute | solution.py:161
  107.1 49.9 %copy-start.34 = (bf16[128,5632]{1,0:T(8,128)(2,1)}, bf16[128,5632]{1,0:T(8,128)(2,1)S(1)}, u32[]{:S(2)}) copy-start(bf16[128,5632]{1,0:T(8,128)(2,1)S(1)} %collective-permute-done.2) | copy-start | bytes 4325380
  107.1 41.5 %collective-permute-start.3 = (bf16[128,5632]{1,0:T(8,128)(2,1)S(1)}, bf16[128,5632]{1,0:T(8,128)(2,1)S(1)}, u32[]{:S(2)}, u32[]{:S(2)}) collective-permute-start(bf16[128,5632]{1,0:T(8,128)(2,1)S(1)} %collective-permute-done.2), channel_id=1, source_target_pairs={{0,1},{1,2},{2,3},{3,4},{4,5},{5,6},{6,7},{7,8},{8,9},{9,10},{10,1... | collective-permute-start | bytes 4325384 | tf_op jit(solution)/shard_map/ppermute | solution.py:159
  123.2 33.7 %collective-permute-start.10 = (bf16[128,5632]{1,0:T(8,128)(2,1)S(1)}, bf16[128,5632]{1,0:T(8,128)(2,1)S(1)}, u32[]{:S(2)}, u32[]{:S(2)}) collective-permute-start(bf16[128,5632]{1,0:T(8,128)(2,1)S(1)} %collective-permute-done.9), channel_id=1, source_target_pairs={{1,0},{2,1},{3,2},{4,3},{5,4},{6,5},{7,6},{8,7},{9,8},{10,9},{11,1... | collective-permute-start | bytes 4325384 | tf_op jit(solution)/shard_map/ppermute | solution.py:161
  148.5 102.5 %copy-start.40 = (bf16[128,5632]{1,0:T(8,128)(2,1)}, bf16[128,5632]{1,0:T(8,128)(2,1)S(1)}, u32[]{:S(2)}) copy-start(bf16[128,5632]{1,0:T(8,128)(2,1)S(1)} %collective-permute-done.3) | copy-start | bytes 4325380
  148.5 34.1 %collective-permute-start.4 = (bf16[128,5632]{1,0:T(8,128)(2,1)S(1)}, bf16[128,5632]{1,0:T(8,128)(2,1)S(1)}, u32[]{:S(2)}, u32[]{:S(2)}) collective-permute-start(bf16[128,5632]{1,0:T(8,128)(2,1)S(1)} %collective-permute-done.3), channel_id=1, source_target_pairs={{0,1},{1,2},{2,3},{3,4},{4,5},{5,6},{6,7},{7,8},{8,9},{9,10},{10,1... | collective-permute-start | bytes 4325384 | tf_op jit(solution)/shard_map/ppermute | solution.py:159
  156.9 37.9 %collective-permute-start.11 = (bf16[128,5632]{1,0:T(8,128)(2,1)S(1)}, bf16[128,5632]{1,0:T(8,128)(2,1)S(1)}, u32[]{:S(2)}, u32[]{:S(2)}) collective-permute-start(bf16[128,5632]{1,0:T(8,128)(2,1)S(1)} %collective-permute-done.10), channel_id=1, source_target_pairs={{1,0},{2,1},{3,2},{4,3},{5,4},{6,5},{7,6},{8,7},{9,8},{10,9},{11,1... | collective-permute-start | bytes 4325384 | tf_op jit(solution)/shard_map/ppermute | solution.py:161
  182.6 68.4 %copy-start.42 = (bf16[128,5632]{1,0:T(8,128)(2,1)}, bf16[128,5632]{1,0:T(8,128)(2,1)S(1)}, u32[]{:S(2)}) copy-start(bf16[128,5632]{1,0:T(8,128)(2,1)S(1)} %collective-permute-done.4) | copy-start | bytes 4325380
  182.6 41.6 %collective-permute-start.5 = (bf16[128,5632]{1,0:T(8,128)(2,1)S(1)}, bf16[128,5632]{1,0:T(8,128)(2,1)S(1)}, u32[]{:S(2)}, u32[]{:S(2)}) collective-permute-start(bf16[128,5632]{1,0:T(8,128)(2,1)S(1)} %collective-permute-done.4), channel_id=1, source_target_pairs={{0,1},{1,2},{2,3},{3,4},{4,5},{5,6},{6,7},{7,8},{8,9},{9,10},{10,1... | collective-permute-start | bytes 4325384 | tf_op jit(solution)/shard_map/ppermute | solution.py:159
  195.9 55.1 %collective-permute-start.12 = (bf16[128,5632]{1,0:T(8,128)(2,1)S(1)}, bf16[128,5632]{1,0:T(8,128)(2,1)}, u32[]{:S(2)}, u32[]{:S(2)}) collective-permute-start(bf16[128,5632]{1,0:T(8,128)(2,1)S(1)} %collective-permute-done.11), channel_id=1, source_target_pairs={{1,0},{2,1},{3,2},{4,3},{5,4},{6,5},{7,6},{8,7},{9,8},{10,9},{11,1... | collective-permute-start | bytes 4325384 | tf_op jit(solution)/shard_map/ppermute | solution.py:161
  224.3 50.7 %copy-start.44 = (bf16[128,5632]{1,0:T(8,128)(2,1)}, bf16[128,5632]{1,0:T(8,128)(2,1)S(1)}, u32[]{:S(2)}) copy-start(bf16[128,5632]{1,0:T(8,128)(2,1)S(1)} %collective-permute-done.5) | copy-start | bytes 4325380
  224.3 50.7 %collective-permute-start.6 = (bf16[128,5632]{1,0:T(8,128)(2,1)S(1)}, bf16[128,5632]{1,0:T(8,128)(2,1)}, u32[]{:S(2)}, u32[]{:S(2)}) collective-permute-start(bf16[128,5632]{1,0:T(8,128)(2,1)S(1)} %collective-permute-done.5), channel_id=1, source_target_pairs={{0,1},{1,2},{2,3},{3,4},{4,5},{5,6},{6,7},{7,8},{8,9},{9,10},{10,1... | collective-permute-start | bytes 4325384 | tf_op jit(solution)/shard_map/ppermute | solution.py:159
  251.0 119.8 %collective-permute-start.13 = (bf16[128,5632]{1,0:T(8,128)(2,1)}, bf16[128,5632]{1,0:T(8,128)(2,1)}, u32[]{:S(2)}, u32[]{:S(2)}) collective-permute-start(bf16[128,5632]{1,0:T(8,128)(2,1)} %collective-permute-done.12), channel_id=1, source_target_pairs={{1,0},{2,1},{3,2},{4,3},{5,4},{6,5},{7,6},{8,7},{9,8},{10,9},{11,1... | collective-permute-start | bytes 4325384 | tf_op jit(solution)/shard_map/ppermute | solution.py:161
  274.9 97.5 %collective-permute-start.7 = (bf16[128,5632]{1,0:T(8,128)(2,1)}, bf16[128,5632]{1,0:T(8,128)(2,1)}, u32[]{:S(2)}, u32[]{:S(2)}) collective-permute-start(bf16[128,5632]{1,0:T(8,128)(2,1)} %collective-permute-done.6), channel_id=1, source_target_pairs={{0,1},{1,2},{2,3},{3,4},{4,5},{5,6},{6,7},{7,8},{8,9},{9,10},{10,1... | collective-permute-start | bytes 4325384 | tf_op jit(solution)/shard_map/ppermute | solution.py:159
  289.3 912.4 %reduce-scatter.5.cloned.1.call-start = ((), (), s32[]{:S(2)}) async-start(), calls=%async_computation.10 | async-start | bytes 24510464 | tf_op jit(solution)/shard_map/reduce_scatter | solution.py:238
  289.8 137.8 %copy-start.64 = (f32[192]{0:T(256)}, f32[192]{0:T(256)S(1)}, u32[]{:S(2)}) copy-start(f32[192]{0:T(256)S(1)} %add_rsqrt_fusion.2) | copy-start | bytes 2308
  289.8 137.7 %copy-start.79 = (f32[192]{0:T(256)}, f32[192]{0:T(256)S(1)}, u32[]{:S(2)}) copy-start(f32[192]{0:T(256)S(1)} %add_convert_fusion) | copy-start | bytes 2308
  370.8 31.5 %collective-permute-start.14 = (bf16[128,5632]{1,0:T(8,128)(2,1)}, bf16[128,5632]{1,0:T(8,128)(2,1)S(1)}, u32[]{:S(2)}, u32[]{:S(2)}) collective-permute-start(bf16[128,5632]{1,0:T(8,128)(2,1)} %collective-permute-done.13), channel_id=1, source_target_pairs={{1,0},{2,1},{3,2},{4,3},{5,4},{6,5},{7,6},{8,7},{9,8},{10,9},{11,1... | collective-permute-start | bytes 4325384 | tf_op jit(solution)/shard_map/ppermute | solution.py:161
  696.4 15.8 copy-start.19
  723.4 1221.1 %reduce-scatter.3.cloned.1.call-start = ((), (), s32[]{:S(2)}) async-start(), calls=%async_computation.9 | async-start | bytes 85229568 | tf_op jit(solution)/shard_map/reduce_scatter | solution.py:235
  767.3 36.7 %copy-start.6 = (f32[192,2048]{1,0:T(8,128)S(1)}, f32[192,2048]{1,0:T(8,128)}, u32[]{:S(2)}) copy-start(f32[192,2048]{1,0:T(8,128)} %copy-done.5) | copy-start | bytes 4718596
  919.4 16.7 copy-start.57
  919.4 16.7 copy-start.58
  919.5 16.7 copy-start.59
  919.5 16.8 copy-start.60
  922.3 14.3 copy-start.56
  953.1 16.2 copy-start.22
  1022.6 21.0 copy-start.24
  1022.6 21.0 copy-start.25
  1201.6 901.5 %all-reduce.33.cloned.1.call-start = ((), (), s32[]{:S(2)}) async-start(), calls=%async_computation.11 | async-start | bytes 12910592 | tf_op jit(solution)/shard_map/psum | solution.py:242
  (66 other events, 262.2 us)
Sparse Core Ops, SparseCore 0:
  10.2 125.7 all-gather.10
  138.2 119.7 all-gather.12
  260.2 96.5 all-gather.14
  358.8 86.2 all-gather.16
  446.5 116.9 all-gather.20
  564.9 118.6 all-gather.18
  685.3 118.6 all-gather.22
  808.1 226.6 reduce-scatter.4
  1201.8 742.7 reduce-scatter.2
  1946.9 156.2 all-reduce.32
